TPU v7x, 128 devices: a whole 4x4x4 slice. The times are simulated.
128 devices in a mesh: fsdp: 32 (over y, z, core), dp: 4 (over x).
Axes of the slice: x: 4, y: 4, z: 4, core: 2. Of those that a mesh axis runs over, the one named last changes fastest.
Arguments:
- tokens: bfloat16 [16384, 4096], P(('fsdp', 'dp')), may hold values from -6 to 6
- gain: float32 [4096], replicated, may hold values from 0.5 to 1.5
- tiles: bfloat16 [512, 128, 128], P('fsdp'), may hold values from -0.25 to 0.25
- tile_rows: int32 [512], replicated, may hold values from 0 to 31, as said below
- tile_cols: int32 [512], replicated, may hold values from 0 to 111, as said below
- cotangent: bfloat16 [16384, 14336], P(('fsdp', 'dp')), may hold values from -6 to 6
Outputs:
- projected: bfloat16 [16384, 14336], P(('fsdp', 'dp'))
- token_grad: bfloat16 [16384, 4096], P(('fsdp', 'dp'))
- tile_grad: float32 [512, 128, 128], P('fsdp')
- gain_grad: float32 [4096], replicated
Inputs may be any that keep to these rules, and one draw needn't show every extreme that they name: The pairs (tile_rows[i], tile_cols[i]) are all different. `tile_cols`: pairs with tile_rows as above.
All inputs are finite; a program needn't handle non-finite values.
Results may differ from a plain program's by a relative error of at most 0.0049.
Values may be sent and summed in bfloat16 or wider, within the bound.
No kernel may reach another device: no remote copies, remote signals or barrier semaphores. Data moves between devices by JAX's collectives and lax.ppermute only.
A program may use at most 256 MiB of HBM per device.

v0:
```python
import jax
import jax.numpy as jnp
from jax import lax
from jax.sharding import PartitionSpec as P


def shards(tokens, gain, tiles, tile_rows, tile_cols, cotangent):
    count = tokens.shape[0]
    width = tokens.shape[1]
    tile = tiles.shape[1]
    row_blocks = width // tile
    col_blocks = cotangent.shape[1] // tile
    x32 = tokens.astype(jnp.float32)
    scale = lax.rsqrt(jnp.mean(x32 * x32, axis=-1, keepdims=True) + 1e-05)
    normed = (x32 * scale * gain).astype(jnp.bfloat16)
    xblocks = normed.reshape(count, row_blocks, tile)
    gblocks = cotangent.reshape(count, col_blocks, tile)
    piece = lax.all_gather(tiles, "fsdp", axis=0, tiled=True)
    rows = tile_rows
    cols = tile_cols
    xsel = jnp.take(xblocks, rows, axis=1)
    gsel = jnp.take(gblocks, cols, axis=1)
    forward = jnp.einsum("tkj,kjm->tkm", xsel, piece, preferred_element_type=jnp.float32)
    backward = jnp.einsum("tkm,kjm->tkj", gsel, piece, preferred_element_type=jnp.float32)
    stacked = jnp.stack([forward, backward], axis=0)
    outsum = jnp.zeros((count, col_blocks, tile), jnp.float32).at[:, tile_cols].add(stacked[0])
    back = jnp.zeros((count, row_blocks, tile), jnp.float32).at[:, tile_rows].add(stacked[1])
    projected = outsum.reshape(count, col_blocks * tile).astype(jnp.bfloat16)
    dnormed = back.reshape(count, width)
    gain_grad = lax.psum(jnp.sum(dnormed * x32 * scale, axis=0), ("fsdp", "dp"))
    inner = jnp.mean(x32 * gain * dnormed, axis=-1, keepdims=True)
    token_grad = (scale * gain * dnormed - x32 * scale**3 * inner).astype(jnp.bfloat16)
    group = tiles.shape[0]
    number = tiles.shape[0] * lax.axis_size("fsdp")

    def group_terms(first):
        rows = lax.dynamic_slice_in_dim(tile_rows, first, group, 0)
        cols = lax.dynamic_slice_in_dim(tile_cols, first, group, 0)
        xsel = jnp.take(xblocks, rows, axis=1)
        gsel = jnp.take(gblocks, cols, axis=1)
        return jnp.einsum("tkj,tkm->kjm", xsel, gsel, preferred_element_type=jnp.float32)

    firsts = group * jnp.arange(number // group, dtype=jnp.int32)
    result = lax.map(group_terms, firsts)
    owned = lax.psum_scatter(
        result.reshape(number, tile, tile), "fsdp", scatter_dimension=0, tiled=True
    )
    tile_grad = lax.psum(owned, "dp")
    return (projected, token_grad, tile_grad, gain_grad)


def solution(mesh):
    placed = (
        P(("fsdp", "dp"), None),
        P(),
        P("fsdp", None, None),
        P(),
        P(),
        P(("fsdp", "dp"), None),
    )
    return jax.shard_map(
        shards,
        mesh=mesh,
        in_specs=placed,
        out_specs=(P(("fsdp", "dp"), None), P(("fsdp", "dp"), None), P("fsdp", None, None), P()),
        check_vma=False,
    )
```

profile of v0, /device:TPU:1, one launch (start us, length us, event | category | flops | bytes accessed | tf_op | source)
XLA Modules:
  0.0 814.4 jit_solution(1176212291491571832)
XLA Ops:
  8.0 6.1 copy.35
  14.0 6.0 copy.36
  21.7 16.2 %gather_fusion.3 = bf16[512,128,128]{2,1,0:T(8,128)(2,1)} fusion(bf16[128,112,128]{2,0,1:T(8,128)(2,1)} %copy.36, s32[1024]{0:T(1024)S(1)} %pad_clamp_fusion.2), kind=kCustom, calls=%fused_computation.3 | custom fusion | bytes 33556480 | tf_op jit(solution)/shard_map/jit(_take)/gather | solution.py:22
  38.5 48.0 %all-gather.2.cloned.1.call-done = bf16[512,128,128]{2,1,0:T(8,128)(2,1)} async-done(((bf16[16,128,128]{2,1,0:T(8,128)(2,1)}), bf16[512,128,128]{2,1,0:T(8,128)(2,1)}) %all-gather.2.cloned.1.call-update) | async-done | bytes 16777232 | tf_op jit(solution)/shard_map/all_gather | solution.py:18
  86.5 28.2 %fusion.9 = f32[512,128,128]{2,1,0:T(8,128)} fusion(bf16[512,128,128]{2,1,0:T(8,128)(2,1)} %all-gather.2.cloned.1.call-done, bf16[512,128,128]{2,1,0:T(8,128)(2,1)} %gather_fusion.3, pred[512]{0:T(512)(128)(4,1)S(1)} %compare_and_fusion.2), kind=kOutput, calls=%fused_computation.22 | convolution fusion | flops 2155872256 | bytes 67109376 | tf_op jit(solution)/shard_map/tkm,kjm->tkj/dot_general | solution.py:24
  115.0 66.1 %scatter_fusion.1 = f32[128,32,128]{2,0,1:T(8,128)S(1)} fusion(f32[128,32,128]{2,0,1:T(8,128)S(1)} %broadcast_in_dim.69, s32[512]{0:T(512)S(1)} %compare_select_fusion.2, f32[512,128,128]{2,1,0:T(8,128)} %fusion.9), kind=kCustom, calls=%fused_computation.5 | custom fusion | flops 8388608 | bytes 100665344 | tf_op jit(solution)/shard_map/scatter-add | solution.py:27
  185.5 2.8 fusion.24
  189.0 237.1 %while.10 = (s32[]{:T(128)}, f32[32,16,128,128]{3,2,1,0:T(8,128)}, s32[32]{0:T(128)S(1)}, s32[512]{0:T(512)S(1)}, bf16[128,32,128]{2,0,1:T(8,128)(2,1)S(1)}, /*i...) while((s32[]{:T(128)}, f32[32,16,128,128]{3,2,1,0:T(8,128)}, ...), condition=%wide.region_5.6_spmd, body=%wide.region_4.5_spmd.sunk | while | flops 67635392 | bytes 4203735 | solution.py:44
  199.0 2.7 gather_fusion
  213.9 2.7 gather_fusion
  228.7 2.7 gather_fusion
  250.9 2.7 gather_fusion
  317.6 2.7 gather_fusion
  325.0 2.7 gather_fusion
  347.2 2.7 gather_fusion
  426.4 15.0 %gather_fusion.2 = bf16[512,128,128]{2,1,0:T(8,128)(2,1)} fusion(bf16[128,32,128]{2,0,1:T(8,128)(2,1)S(1)} %get-tuple-element.182, s32[1024]{0:T(1024)S(1)} %pad_clamp_fusion.3), kind=kCustom, calls=%fused_computation.2 | custom fusion | bytes 33556480 | tf_op jit(solution)/shard_map/jit(_take)/gather | solution.py:21
  441.3 148.6 %reduce-scatter.2.cloned.1.call-done = f32[16,128,128]{2,1,0:T(8,128)} async-done(((f32[512,128,128]{2,1,0:T(8,128)}), f32[16,128,128]{2,1,0:T(8,128)}) %reduce-scatter.2.cloned.1.call-update) | async-done | bytes 1048592 | tf_op jit(solution)/shard_map/reduce_scatter | solution.py:45
  590.0 24.5 %fusion.11 = f32[512,128,128]{2,1,0:T(8,128)} fusion(bf16[512,128,128]{2,1,0:T(8,128)(2,1)} %all-gather.2.cloned.1.call-done, bf16[512,128,128]{2,1,0:T(8,128)(2,1)} %gather_fusion.2, pred[512]{0:T(512)(128)(4,1)S(1)} %compare_and_fusion.3), kind=kOutput, calls=%fused_computation.24 | convolution fusion | flops 2155872256 | bytes 67109376 | tf_op jit(solution)/shard_map/tkj,kjm->tkm/dot_general | solution.py:23
  614.5 3.8 broadcast_in_dim.64
  618.3 103.4 %scatter_fusion = f32[128,112,128]{2,0,1:T(8,128)} fusion(f32[128,112,128]{2,0,1:T(8,128)} %broadcast_in_dim.64, s32[512]{0:T(512)S(1)} %compare_select_fusion.3, f32[512,128,128]{2,1,0:T(8,128)} %fusion.11), kind=kCustom, calls=%fused_computation.4 | custom fusion | flops 8388608 | bytes 100665344 | tf_op jit(solution)/shard_map/scatter-add | solution.py:26
  721.7 5.8 convert_element_type.17
  727.5 6.1 copy.34
  733.6 6.1 copy.40
  741.0 64.6 %psum.15 = f32[4096]{0:T(1024)} all-reduce(f32[4096]{0:T(1024)S(1)} %get-tuple-element.68), channel_id=1, replica_groups=mesh['fsdp'=32,'dp'=4] {'fsdp','dp'}, use_global_device_ids=true, to_apply=%region_9.10 | all-reduce | flops 4096 | bytes 32768 | tf_op jit(solution)/shard_map/psum | solution.py:30
  (250 shorter events, 167.2 us)
Async XLA Ops:
  7.2 14.5 %copy-start.2 = (s32[512]{0:T(512)S(1)}, s32[512]{0:T(512)}, u32[]{:S(2)}) copy-start(s32[512]{0:T(512)} %param.12) | copy-start | bytes 6148
  7.2 79.4 %all-gather.2.cloned.1.call-start = ((), (), s32[]{:S(2)}) async-start(), calls=%async_computation.1 | async-start | bytes 17301504 | tf_op jit(solution)/shard_map/all_gather | solution.py:18
  7.9 582.1 %reduce-scatter.2.cloned.1.call-start = ((), (), s32[]{:S(2)}) async-start(), calls=%async_computation.2 | async-start | bytes 34603008 | tf_op jit(solution)/shard_map/reduce_scatter | solution.py:45
  21.7 16.8 %copy-start.3 = (s32[512]{0:T(512)S(1)}, s32[512]{0:T(512)}, u32[]{:S(2)}) copy-start(s32[512]{0:T(512)} %param.11) | copy-start | bytes 6148
  115.0 68.0 %copy-start.1 = (f32[4096]{0:T(1024)S(1)}, f32[4096]{0:T(1024)}, u32[]{:S(2)}) copy-start(f32[4096]{0:T(1024)} %param.9) | copy-start | bytes 49156
  426.1 379.5 %all-reduce.2.cloned.1.call-start = ((), (), s32[]{:S(2)}) async-start(), calls=%async_computation.3 | async-start | bytes 2097152 | tf_op jit(solution)/shard_map/psum | solution.py:48
  721.7 18.0 %copy-start = (bf16[128,4096]{0,1:T(8,128)(2,1)S(1)}, bf16[128,4096]{0,1:T(8,128)(2,1)}, u32[]{:S(2)}) copy-start(bf16[128,4096]{0,1:T(8,128)(2,1)} %get-tuple-element.90) | copy-start | bytes 3145732
Sparse Core Ops, SparseCore 0:
  10.3 76.2 all-gather.1
  426.2 163.6 reduce-scatter.1
  592.5 44.0 all-reduce.1
where the time goes:
time: 820 us; the launch traced here: 814 us
  waiting for transfers between devices  197 us (24%)
  local copies, waits for them, and re-layouts  192 us (23%)
  other arithmetic  184 us (22%)
  matrix products  98.3 us (12%)
  blocking collectives  64.6 us (8%)
  loops' own time  63.1 us (8%)
  between operations  13.9 us (2%)
    reduce_scatter x1, waiting for transfers between devices, shards(): lax.psum_scatter(result.reshape(number, tile, tile), 'fsdp', scatter_dime...  149 us
    scatter-add x1, other arithmetic, shards(): jnp.zeros((count, col_blocks, tile), jnp.float32).at[:, tile_cols]  103 us
    gather x32, local copies, waits for them, and re-layouts, group_terms(): gsel = jnp.take(gblocks, cols, axis=1)  85.9 us
    scatter-add x1, other arithmetic, shards(): jnp.zeros((count, row_blocks, tile), jnp.float32).at[:, tile_rows]  66.1 us
    psum x1, blocking collectives, shards(): gain_grad = lax.psum(jnp.sum(dnormed * x32 * scale, axis=0), ('fsdp', 'dp'))  64.6 us
    another operation x1, loops' own time, shards(): result = lax.map(group_terms, firsts)  63.1 us
    all_gather x1, waiting for transfers between devices, shards(): piece = lax.all_gather(tiles, 'fsdp', axis=0, tiled=True)  48 us
    dot_general x32, matrix products, group_terms(): jnp.einsum('tkj,tkm->kjm', xsel, gsel, preferred_element_type=jnp.float32)  45.6 us
  transfers between devices with their start and end apart: 3, of which 2 were waited for; matrix products, arithmetic and copies ran while one was open for 24% of the time, Pallas kernels for 0%

commit v1 on v0

--- a/solution.py
+++ b/solution.py
@@ -27,7 +27,9 @@
     back = jnp.zeros((count, row_blocks, tile), jnp.float32).at[:, tile_rows].add(stacked[1])
     projected = outsum.reshape(count, col_blocks * tile).astype(jnp.bfloat16)
     dnormed = back.reshape(count, width)
-    gain_grad = lax.psum(jnp.sum(dnormed * x32 * scale, axis=0), ("fsdp", "dp"))
+    gain_grad = jnp.sum(
+        lax.all_gather(jnp.sum(dnormed * x32 * scale, axis=0), ("fsdp", "dp")), axis=0
+    )
     inner = jnp.mean(x32 * gain * dnormed, axis=-1, keepdims=True)
     token_grad = (scale * gain * dnormed - x32 * scale**3 * inner).astype(jnp.bfloat16)
     group = tiles.shape[0]

time: 820 us -> 758 us (0.924)
  blocking collectives: 64.6 us -> 0 us
    psum x1 -> x0, blocking collectives: 64.6 us -> none  [shards(): gain_grad = lax.psum(jnp.sum(dnormed * x32 * scale, axis=0), ('fsdp', 'dp'))]
    unnamed x13 -> x15, local copies, waits for them, and re-layouts: 17.4 us -> 16.4 us
  transfers between devices with their start and end apart: 3 -> 4, of which waited for: 2 -> 2; matrix products, arithmetic and copies ran while one was open for 24% -> 26% of each run, Pallas kernels for 0% -> 0%
where the time goes in v1:
time: 758 us; the launch traced here: 753 us
  waiting for transfers between devices  198 us (26%)
  local copies, waits for them, and re-layouts  193 us (25%)
  other arithmetic  186 us (25%)
  matrix products  98.3 us (13%)
  loops' own time  63.1 us (8%)
  between operations  13.9 us (2%)
    reduce_scatter x1, waiting for transfers between devices, shards(): lax.psum_scatter(result.reshape(number, tile, tile), 'fsdp', scatter_dime...  148 us
    scatter-add x1, other arithmetic, shards(): jnp.zeros((count, col_blocks, tile), jnp.float32).at[:, tile_cols]  104 us
    gather x32, local copies, waits for them, and re-layouts, group_terms(): gsel = jnp.take(gblocks, cols, axis=1)  85.9 us
    scatter-add x1, other arithmetic, shards(): jnp.zeros((count, row_blocks, tile), jnp.float32).at[:, tile_rows]  66.1 us
    another operation x1, loops' own time, shards(): result = lax.map(group_terms, firsts)  63.1 us
    all_gather x1, waiting for transfers between devices, shards(): piece = lax.all_gather(tiles, 'fsdp', axis=0, tiled=True)  49.1 us
    dot_general x32, matrix products, group_terms(): jnp.einsum('tkj,tkm->kjm', xsel, gsel, preferred_element_type=jnp.float32)  45.6 us
    dot_general x1, matrix products, shards(): jnp.einsum('tkm,kjm->tkj', gsel, piece, preferred_element_type=jnp.float32)  28.2 us
  transfers between devices with their start and end apart: 4, of which 2 were waited for; matrix products, arithmetic and copies ran while one was open for 26% of the time, Pallas kernels for 0%

profile of v1, /device:TPU:1, one launch (start us, length us, event | category | flops | bytes accessed | tf_op | source)
XLA Modules:
  0.0 753.0 jit_solution(3270237624664294753)
XLA Ops:
  8.0 6.1 copy.46
  14.0 6.0 copy.47
  20.8 16.1 %gather_fusion.3 = bf16[512,128,128]{2,1,0:T(8,128)(2,1)} fusion(bf16[128,112,128]{2,0,1:T(8,128)(2,1)} %copy.47, s32[1024]{0:T(1024)S(1)} %pad_clamp_fusion.2), kind=kCustom, calls=%fused_computation.3 | custom fusion | bytes 33556480 | tf_op jit(solution)/shard_map/jit(_take)/gather | solution.py:22
  37.5 49.1 %all-gather.4.cloned.1.call-done = bf16[512,128,128]{2,1,0:T(8,128)(2,1)} async-done(((bf16[16,128,128]{2,1,0:T(8,128)(2,1)}), bf16[512,128,128]{2,1,0:T(8,128)(2,1)}) %all-gather.4.cloned.1.call-update) | async-done | bytes 16777232 | tf_op jit(solution)/shard_map/all_gather | solution.py:18
  86.6 28.2 %fusion.9 = f32[512,128,128]{2,1,0:T(8,128)} fusion(bf16[512,128,128]{2,1,0:T(8,128)(2,1)} %all-gather.4.cloned.1.call-done, bf16[512,128,128]{2,1,0:T(8,128)(2,1)} %gather_fusion.3, pred[512]{0:T(512)(128)(4,1)S(1)} %compare_and_fusion.2), kind=kOutput, calls=%fused_computation.22 | convolution fusion | flops 2155872256 | bytes 67109376 | tf_op jit(solution)/shard_map/tkm,kjm->tkj/dot_general | solution.py:24
  115.0 66.1 %scatter_fusion.1 = f32[128,32,128]{2,0,1:T(8,128)S(1)} fusion(f32[128,32,128]{2,0,1:T(8,128)S(1)} %broadcast_in_dim.69, s32[512]{0:T(512)S(1)} %compare_select_fusion.2, f32[512,128,128]{2,1,0:T(8,128)} %fusion.9), kind=kCustom, calls=%fused_computation.5 | custom fusion | flops 8388608 | bytes 100665344 | tf_op jit(solution)/shard_map/scatter-add | solution.py:27
  183.0 3.1 fusion.28
  186.1 2.8 fusion.24
  189.6 237.1 %while.10 = (s32[]{:T(128)}, f32[32,16,128,128]{3,2,1,0:T(8,128)}, s32[32]{0:T(128)S(1)}, s32[512]{0:T(512)S(1)}, bf16[128,32,128]{2,0,1:T(8,128)(2,1)S(1)}, /*i...) while((s32[]{:T(128)}, f32[32,16,128,128]{3,2,1,0:T(8,128)}, ...), condition=%wide.region_5.6_spmd, body=%wide.region_4.5_spmd.sunk | while | flops 67635392 | bytes 4203735 | solution.py:46
  192.2 2.7 gather_fusion
  199.6 2.7 gather_fusion
  214.5 2.7 gather_fusion
  221.9 2.7 gather_fusion
  229.2 2.7 gather_fusion
  236.7 2.7 gather_fusion
  266.3 2.7 gather_fusion
  427.7 15.0 %gather_fusion.2 = bf16[512,128,128]{2,1,0:T(8,128)(2,1)} fusion(bf16[128,32,128]{2,0,1:T(8,128)(2,1)S(1)} %get-tuple-element.194, s32[1024]{0:T(1024)S(1)} %pad_clamp_fusion.3), kind=kCustom, calls=%fused_computation.2 | custom fusion | bytes 33556480 | tf_op jit(solution)/shard_map/jit(_take)/gather | solution.py:21
  442.6 147.7 %reduce-scatter.2.cloned.1.call-done = f32[16,128,128]{2,1,0:T(8,128)} async-done(((f32[512,128,128]{2,1,0:T(8,128)}), f32[16,128,128]{2,1,0:T(8,128)}) %reduce-scatter.2.cloned.1.call-update) | async-done | bytes 1048592 | tf_op jit(solution)/shard_map/reduce_scatter | solution.py:47
  590.4 24.4 %fusion.11 = f32[512,128,128]{2,1,0:T(8,128)} fusion(bf16[512,128,128]{2,1,0:T(8,128)(2,1)} %all-gather.4.cloned.1.call-done, bf16[512,128,128]{2,1,0:T(8,128)(2,1)} %gather_fusion.2, pred[512]{0:T(512)(128)(4,1)S(1)} %compare_and_fusion.3), kind=kOutput, calls=%fused_computation.24 | convolution fusion | flops 2155872256 | bytes 67109376 | tf_op jit(solution)/shard_map/tkj,kjm->tkm/dot_general | solution.py:23
  614.8 3.8 broadcast_in_dim.64
  618.7 103.7 %scatter_fusion = f32[128,112,128]{2,0,1:T(8,128)} fusion(f32[128,112,128]{2,0,1:T(8,128)} %broadcast_in_dim.64, s32[512]{0:T(512)S(1)} %compare_select_fusion.3, f32[512,128,128]{2,1,0:T(8,128)} %fusion.11), kind=kCustom, calls=%fused_computation.4 | custom fusion | flops 8388608 | bytes 100665344 | tf_op jit(solution)/shard_map/scatter-add | solution.py:26
  722.4 5.8 convert_element_type.17
  728.1 6.2 copy.45
  734.3 6.1 copy.51
  (256 shorter events, 166.9 us)
Async XLA Ops:
  7.2 12.9 %copy-start.1 = (bf16[128,4096]{1,0:T(8,128)(2,1)S(1)}, bf16[128,4096]{1,0:T(8,128)(2,1)}, u32[]{:S(2)}) copy-start(bf16[128,4096]{1,0:T(8,128)(2,1)} %param.8) | copy-start | bytes 3145732
  7.2 79.4 %all-gather.4.cloned.1.call-start = ((), (), s32[]{:S(2)}) async-start(), calls=%async_computation.1 | async-start | bytes 17301504 | tf_op jit(solution)/shard_map/all_gather | solution.py:18
  7.9 582.5 %reduce-scatter.2.cloned.1.call-start = ((), (), s32[]{:S(2)}) async-start(), calls=%async_computation.2 | async-start | bytes 34603008 | tf_op jit(solution)/shard_map/reduce_scatter | solution.py:47
  8.0 12.8 %copy-start.3 = (s32[512]{0:T(512)S(1)}, s32[512]{0:T(512)}, u32[]{:S(2)}) copy-start(s32[512]{0:T(512)} %param.12) | copy-start | bytes 6148
  20.8 16.7 %copy-start.4 = (s32[512]{0:T(512)S(1)}, s32[512]{0:T(512)}, u32[]{:S(2)}) copy-start(s32[512]{0:T(512)} %param.11) | copy-start | bytes 6148
  115.0 68.0 %copy-start.2 = (f32[4096]{0:T(1024)S(1)}, f32[4096]{0:T(1024)}, u32[]{:S(2)}) copy-start(f32[4096]{0:T(1024)} %param.9) | copy-start | bytes 49156
  426.7 315.0 %all-gather.6.cloned.1.call-start = ((), (), s32[]{:S(2)}) async-start(), calls=%async_computation.4 | async-start | bytes 2113536 | tf_op jit(solution)/shard_map/all_gather | solution.py:31
  427.4 316.7 %all-reduce.2.cloned.1.call-start = ((), (), s32[]{:S(2)}) async-start(), calls=%async_computation.3 | async-start | bytes 2097152 | tf_op jit(solution)/shard_map/psum | solution.py:50
  728.1 12.2 %copy-start = (bf16[128,4096]{0,1:T(8,128)(2,1)S(1)}, bf16[128,4096]{0,1:T(8,128)(2,1)}, u32[]{:S(2)}) copy-start(bf16[128,4096]{0,1:T(8,128)(2,1)} %get-tuple-element.101) | copy-start | bytes 3145732
Sparse Core Ops, SparseCore 0:
  10.3 76.2 all-gather.3
  426.8 163.5 reduce-scatter.1
  594.4 65.5 all-gather.5
  662.3 41.3 all-reduce.1
